TPU v7x, 32 devices: a whole 2x2x4 slice. The times are simulated.
32 devices in a mesh: group: 2 (over x), seq: 16 (over z, y, core).
Axes of the slice: x: 2, y: 2, z: 4, core: 2. Of those that a mesh axis runs over, the one named last changes fastest.
Arguments:
- x_rows: bfloat16 [32, 8192], P('group', 'seq'), parts along dimension 0, may hold values from -0.59765625 to 0.59765625
- attn_gain: bfloat16 [8192], replicated, may hold values from 0.5 to 1.5
- q_weight: bfloat16 [8192, 8192], P(None, 'seq'), may hold values from -0.0625 to 0.0625
- o_weight: bfloat16 [8192, 8192], P('seq'), may hold values from -0.0625 to 0.0625
- mlp_gain: bfloat16 [8192], replicated, may hold values from 0.5 to 1.5
- gate_weight: bfloat16 [8192, 14336], P(None, 'seq'), may hold values from -0.0625 to 0.0625
- up_weight: bfloat16 [8192, 14336], P(None, 'seq'), may hold values from -0.0625 to 0.0625
- down_weight: bfloat16 [14336, 8192], P('seq'), may hold values from -0.046875 to 0.046875
- kv_cache: bfloat16 [2, 4096, 1024], P(None, ('group', 'seq')), parts along dimension 1, may hold values from -250 to 250, as said below
- block_mask: int32 [32, 8, 16], P('group', None, 'seq'), parts along dimension 0, may hold values from 0 to 1, as said below
Outputs:
- y_rows: bfloat16 [32, 8192], P('group', 'seq'), parts along dimension 0
There are 2 independent parts, one for each index of `group`. A program takes and returns all parts, laid end to end along the dimension named above; an argument that names none is the same for every part. Nothing has to cross between parts.
Inputs may be any that keep to these rules, and one draw needn't show every extreme that they name: `kv_cache`: document keys and values; they differ from document to document. `block_mask`: 1 where the row may attend to that block of 128 document tokens for that key-value head, else 0; the document's last block is 1 for every row and key-value head.
All inputs are finite; a program needn't handle non-finite values.
Results may differ from a plain program's by a relative error of at most 0.013.
The roundings to bfloat16 on the way count: a program that leaves them out, or rounds other values in their place, can miss the bound.
Values may be sent and summed in bfloat16 or wider, within the bound.
A program may use at most 192 MiB of HBM per device.

v0:
```python
import functools

import jax
import jax.numpy as jnp
from jax import lax
from jax.experimental import pallas as pl
from jax.experimental.pallas import tpu as pltpu
from jax.sharding import PartitionSpec as P

HEADS = 64
KV_HEADS = 8
HEAD_DIM = 128
BLOCK = 128


eps = 1e-05
floor_score = -1e30


def combined_all(x, axis, combine):
    everything = jax.tree.map(lambda part: lax.all_gather(part, axis), x)
    initial = jax.tree.map(lambda part: part[0], everything)

    def turn(k, so_far):
        return combine(so_far, jax.tree.map(lambda part: part[k], everything))

    return lax.fori_loop(1, lax.axis_size(axis), turn, initial)


def rms_norm(values, gain):
    wide = values.astype(jnp.float32)
    inverse = lax.rsqrt(jnp.mean(wide * wide, axis=-1, keepdims=True) + eps)
    return (wide * inverse * gain.astype(jnp.float32)).astype(jnp.bfloat16)


def combine_states(first, second):
    top_a, total_a, accum_a = first
    top_b, total_b, accum_b = second
    top = jnp.maximum(top_a, top_b)
    factor_a = jnp.exp(top_a - top)
    factor_b = jnp.exp(top_b - top)
    return (
        top,
        total_a * factor_a + total_b * factor_b,
        accum_a * factor_a[..., None] + accum_b * factor_b[..., None],
    )


def local(
    x_rows,
    attn_gain,
    q_weight,
    o_weight,
    mlp_gain,
    gate_weight,
    up_weight,
    down_weight,
    kv_cache,
    block_mask,
):
    rows = x_rows.shape[0]
    group = HEADS // KV_HEADS
    key_len = kv_cache.shape[1]
    spans = key_len // BLOCK
    scale = 1.0 / HEAD_DIM**0.5
    whole = lax.all_gather(x_rows, "seq", axis=1, tiled=True)
    normed = rms_norm(whole, attn_gain)
    query_part = jnp.dot(normed, q_weight, preferred_element_type=jnp.float32).astype(jnp.bfloat16)
    queries = lax.all_gather(query_part, "seq", axis=1, tiled=True)
    doc_keys = kv_cache[0]
    doc_values = kv_cache[1]

    def one_group(index):
        query_group = lax.dynamic_slice_in_dim(
            queries, index * (group * HEAD_DIM), group * HEAD_DIM, 1
        ).reshape(rows, group, HEAD_DIM)
        key_group = lax.dynamic_slice_in_dim(doc_keys, index * HEAD_DIM, HEAD_DIM, 1)
        value_group = lax.dynamic_slice_in_dim(doc_values, index * HEAD_DIM, HEAD_DIM, 1)
        mask_group = lax.dynamic_slice_in_dim(block_mask, index, 1, 1)[:, 0, :]
        scores = (
            jnp.einsum("rhd,kd->rhk", query_group, key_group, preferred_element_type=jnp.float32)
            * scale
        )
        scores = scores.reshape(rows, group, spans, BLOCK)
        live = (mask_group == 1)[:, None, :, None]
        masked = jnp.where(live, scores, floor_score)
        local_top = jnp.max(masked, axis=(2, 3))
        weights = jnp.where(live, jnp.exp(masked - local_top[..., None, None]), 0.0)
        local_total = jnp.sum(weights, axis=(2, 3))
        rounded = weights.astype(jnp.bfloat16).reshape(rows, group, key_len)
        local_accum = jnp.einsum(
            "rhk,kd->rhd", rounded, value_group, preferred_element_type=jnp.float32
        )
        return (local_top, local_total, local_accum)

    tops, totals, accums = lax.map(one_group, jnp.arange(KV_HEADS, dtype=jnp.int32))
    local_top = jnp.moveaxis(tops, 0, 1)
    local_total = jnp.moveaxis(totals, 0, 1)
    local_accum = jnp.moveaxis(accums, 0, 1)
    columns = q_weight.shape[1]
    col_start = lax.axis_index("seq") * columns
    top, total, accum = combined_all((local_top, local_total, local_accum), "seq", combine_states)
    attended = accum / total[..., None]
    attended = attended.reshape(rows, HEADS * HEAD_DIM).astype(jnp.bfloat16)
    attn_cols = lax.dynamic_slice_in_dim(attended, col_start, columns, 1)
    weight_cols = o_weight
    attn_out = lax.psum_scatter(
        lax.dot_general(
            weight_cols, attn_cols, (((0,), (1,)), ((), ())), preferred_element_type=jnp.float32
        ),
        "seq",
        scatter_dimension=0,
        tiled=True,
    )
    stream = (x_rows.astype(jnp.float32) + attn_out.T).astype(jnp.bfloat16)
    stream_whole = lax.all_gather(stream, "seq", axis=1, tiled=True)
    normed_two = rms_norm(stream_whole, mlp_gain)
    gate = jnp.dot(normed_two, gate_weight, preferred_element_type=jnp.float32)
    upward = jnp.dot(normed_two, up_weight, preferred_element_type=jnp.float32)
    hidden = (jax.nn.silu(gate) * upward).astype(jnp.bfloat16)
    weight_cols = down_weight
    down_out = lax.psum_scatter(
        lax.dot_general(
            weight_cols, hidden, (((0,), (1,)), ((), ())), preferred_element_type=jnp.float32
        ),
        "seq",
        scatter_dimension=0,
        tiled=True,
    )
    return (stream.astype(jnp.float32) + down_out.T).astype(jnp.bfloat16)


FAR_FIRST = (4, 3, 5, 2, 6, 1, 7)
SCALE = 1.0 / HEAD_DIM**0.5


def layer_kernel(
    x_ref,
    attn_gain,
    q_hbm,
    o_hbm,
    mlp_gain,
    gate_hbm,
    up_hbm,
    down_hbm,
    kv_hbm,
    mask_ref,
    y_ref,
    q_w,
    o_w,
    gate_w,
    up_w,
    down_w,
    x_all,
    s_all,
    normed,
    stream_ref,
    kv_all,
    mask_out,
    mask_all,
    scores,
    part_one,
    got_one,
    part_two,
    got_two,
    own_ref,
    w_sem,
    kv_own_sem,
    x_send,
    x_recv,
    x_pass,
    s_send,
    s_recv,
    s_pass,
    kv_send,
    kv_recv,
    kv_pass,
    m_send,
    m_recv,
    m_pass,
    one_send,
    one_recv,
    two_send,
    two_recv,
):
    devices, rows, cols = x_all.shape
    chips = devices // 2
    group = cols // HEAD_DIM
    me = lax.axis_index("seq")
    chip = me // 2
    core = me % 2
    partner = chip * 2 + 1 - core

    def fetch(k, src, dst):
        return pltpu.make_async_copy(src, dst, w_sem.at[k])

    def remote(src, dst, send, recv, device):
        return pltpu.make_async_remote_copy(
            src_ref=src,
            dst_ref=dst,
            send_sem=send,
            recv_sem=recv,
            device_id={"seq": device},
            device_id_type=pl.DeviceIdType.MESH,
        )

    def chip_at(off):
        return (chip + off) % chips

    def gather_start(src, dst, send, recv):
        for off in FAR_FIRST:
            remote(src, dst.at[me], send.at[off], recv.at[me], chip_at(off) * 2 + core).start()
        remote(src, dst.at[me], send.at[0], recv.at[me], partner).start()

    def gather_pass(dst, send, recv, hand):
        for off in reversed(FAR_FIRST):
            other = chip_at(off) * 2 + core
            remote(dst.at[other], dst.at[other], send.at[off], recv.at[other], partner).wait_recv()
            remote(dst.at[other], dst.at[other], hand.at[off], recv.at[other], partner).start()

    def gather_finish(dst, send, recv):
        for off in range(chips):
            other = chip_at(off) * 2 + 1 - core
            remote(dst.at[other], dst.at[other], send.at[0], recv.at[other], partner).wait_recv()

    def gather_drain(src, dst, send, recv, hand):
        for off in range(chips):
            remote(src, dst.at[me], send.at[off], recv.at[me], partner).wait_send()
        for off in FAR_FIRST:
            remote(src, dst.at[me], hand.at[off], recv.at[me], partner).wait_send()

    fetch_q = fetch(0, q_hbm, q_w)
    fetch_o = fetch(1, o_hbm, o_w)
    fetch_gate = fetch(2, gate_hbm, gate_w)
    fetch_up = fetch(3, up_hbm, up_w)
    fetch_down = fetch(4, down_hbm, down_w)

    barrier = pltpu.get_barrier_semaphore()
    for off in range(1, devices):
        pl.semaphore_signal(
            barrier,
            inc=1,
            device_id={"seq": (me + off) % devices},
            device_id_type=pl.DeviceIdType.MESH,
        )
    fetch_q.start()
    own_kv = pltpu.make_async_copy(
        kv_hbm.at[:, :, pl.ds(pl.multiple_of(chip * HEAD_DIM, HEAD_DIM), HEAD_DIM)],
        kv_all.at[me],
        kv_own_sem,
    )
    own_kv.start()
    fetch_o.start()
    for g in range(KV_HEADS):
        mask_out[g] = jnp.broadcast_to(
            mask_ref[:, g : g + 1].astype(jnp.float32), (rows, HEAD_DIM)
        )
    mask_all[me] = mask_out[chip]
    x_all[me] = x_ref[...]
    pl.semaphore_wait(barrier, devices - 1)

    gather_start(x_ref, x_all, x_send, x_recv)

    def kv_of(where):
        return kv_hbm.at[:, :, pl.ds(pl.multiple_of(where * HEAD_DIM, HEAD_DIM), HEAD_DIM)]

    for off in FAR_FIRST:
        there = chip_at(off)
        to = there * 2 + core
        remote(kv_of(there), kv_all.at[me], kv_send.at[off], kv_recv.at[me], to).start()
        remote(mask_out.at[there], mask_all.at[me], m_send.at[off], m_recv.at[me], to).start()
    remote(kv_of(chip), kv_all.at[me], kv_send.at[0], kv_recv.at[me], partner).start()
    remote(mask_out.at[chip], mask_all.at[me], m_send.at[0], m_recv.at[me], partner).start()
    fetch_gate.start()
    fetch_up.start()
    fetch_down.start()

    def norm(values, gain):
        squares = jnp.zeros((rows, cols), jnp.float32)
        for i in range(devices):
            wide = values[i].astype(jnp.float32)
            squares = squares + wide * wide
        mean = jnp.sum(squares, axis=-1, keepdims=True) * (1.0 / (devices * cols))
        inverse = lax.rsqrt(mean + eps)
        for i in range(devices):
            part_gain = gain[i * cols : (i + 1) * cols].astype(jnp.float32).reshape(1, cols)
            normed[i] = (values[i].astype(jnp.float32) * inverse * part_gain).astype(jnp.bfloat16)

    gather_pass(x_all, x_send, x_recv, x_pass)
    gather_finish(x_all, x_send, x_recv)
    norm(x_all, attn_gain)
    fetch_q.wait()
    step = 4

    def q_step(t, total):
        for u in range(step):
            i = t * step + u
            total = total + jnp.dot(
                normed[i],
                q_w[pl.ds(pl.multiple_of(i * cols, cols), cols), :],
                preferred_element_type=jnp.float32,
            )
        return total

    queries = lax.fori_loop(
        0, devices // step, q_step, jnp.zeros((rows, cols), jnp.float32)
    ).astype(jnp.bfloat16)
    query = jnp.concatenate(
        [queries[:, h * HEAD_DIM : (h + 1) * HEAD_DIM] for h in range(group)], axis=0
    )

    gather_pass(kv_all, kv_send, kv_recv, kv_pass)
    gather_pass(mask_all, m_send, m_recv, m_pass)
    own_kv.wait()
    gather_finish(kv_all, kv_send, kv_recv)
    gather_finish(mask_all, m_send, m_recv)

    def live_at(c):
        return jnp.concatenate([mask_all[c]] * group, axis=0) > 0.5

    tops = []
    for c in range(devices):
        score = (
            lax.dot_general(
                query,
                kv_all[c, 0],
                (((1,), (1,)), ((), ())),
                preferred_element_type=jnp.float32,
            )
            * SCALE
        )
        masked = jnp.where(live_at(c), score, floor_score)
        scores[c] = masked
        tops.append(jnp.max(masked, axis=-1, keepdims=True))
    top = functools.reduce(jnp.maximum, tops)
    total = jnp.zeros((group * rows, 1), jnp.float32)
    accum = jnp.zeros((group * rows, HEAD_DIM), jnp.float32)
    for c in range(devices):
        weight = jnp.where(live_at(c), jnp.exp(scores[c] - tops[c]), 0.0)
        factor = jnp.exp(tops[c] - top)
        total = total + factor * jnp.sum(weight, axis=-1, keepdims=True)
        accum = accum + factor * jnp.dot(
            weight.astype(jnp.bfloat16), kv_all[c, 1], preferred_element_type=jnp.float32
        )
    ratio = accum / total
    attended = jnp.concatenate(
        [ratio[h * rows : (h + 1) * rows] for h in range(group)], axis=1
    ).astype(jnp.bfloat16)

    def scatter(values, weight, part, got, send, recv):
        def target(s):
            off = devices // 2 + ((s + 1) // 2) * (1 - 2 * (s % 2))
            return (me + off) % devices

        def post(s):
            to = target(s)
            remote(part.at[to], got.at[me], send.at[s], recv.at[me], to).start()

        def product(s):
            to = target(s)
            return jnp.dot(
                values,
                weight[:, pl.ds(pl.multiple_of(to * cols, cols), cols)],
                preferred_element_type=jnp.float32,
            )

        def turn(t, _):
            first = product(2 * t)
            second = product(2 * t + 1)
            part[target(2 * t)] = first.astype(part.dtype)
            part[target(2 * t + 1)] = second.astype(part.dtype)
            own_ref[...] = second

            @pl.when(t > 0)
            def _():
                post(2 * t - 2)
                post(2 * t - 1)

            return 0

        lax.fori_loop(0, devices // 2, turn, 0)
        post(devices - 2)

        def add(s, total):
            other = target(devices - 2 - s)
            remote(part.at[other], got.at[other], send.at[s], recv.at[other], other).wait_recv()
            return total + got[other].astype(jnp.float32)

        return lax.fori_loop(0, devices - 1, add, own_ref[...])

    def scatter_drain(part, got, send, recv):
        for s in range(devices - 1):
            remote(part.at[0], got.at[me], send.at[s], recv.at[me], partner).wait_send()

    fetch_o.wait()
    attn_out = scatter(attended, o_w, part_one, got_one, one_send, one_recv)
    stream = (x_ref[...].astype(jnp.float32) + attn_out).astype(jnp.bfloat16)
    stream_ref[...] = stream
    s_all[me] = stream
    gather_start(stream_ref, s_all, s_send, s_recv)
    gather_pass(s_all, s_send, s_recv, s_pass)
    gather_finish(s_all, s_send, s_recv)
    norm(s_all, mlp_gain)
    fetch_gate.wait()
    fetch_up.wait()
    wide = gate_w.shape[1]

    def ff_step(t, sums):
        gate, upward = sums
        for u in range(2):
            i = t * 2 + u
            at = pl.ds(pl.multiple_of(i * cols, cols), cols)
            gate = gate + jnp.dot(normed[i], gate_w[at, :], preferred_element_type=jnp.float32)
            upward = upward + jnp.dot(normed[i], up_w[at, :], preferred_element_type=jnp.float32)
        return gate, upward

    zeros = jnp.zeros((rows, wide), jnp.float32)
    gate, upward = lax.fori_loop(0, devices // 2, ff_step, (zeros, zeros))
    hidden = (gate / (1.0 + jnp.exp(-gate)) * upward).astype(jnp.bfloat16)
    fetch_down.wait()
    down_out = scatter(hidden, down_w, part_two, got_two, two_send, two_recv)
    y_ref[...] = (stream_ref[...].astype(jnp.float32) + down_out).astype(jnp.bfloat16)

    gather_drain(x_ref, x_all, x_send, x_recv, x_pass)
    gather_drain(kv_of(chip), kv_all, kv_send, kv_recv, kv_pass)
    gather_drain(mask_out.at[0], mask_all, m_send, m_recv, m_pass)
    gather_drain(stream_ref, s_all, s_send, s_recv, s_pass)
    scatter_drain(part_one, got_one, one_send, one_recv)
    scatter_drain(part_two, got_two, two_send, two_recv)


def layer(
    x_rows,
    attn_gain,
    q_weight,
    o_weight,
    mlp_gain,
    gate_weight,
    up_weight,
    down_weight,
    kv_cache,
    block_mask,
):
    rows, cols = x_rows.shape
    devices = lax.axis_size("seq")
    chips = devices // 2
    wide = gate_weight.shape[1]
    dma = pltpu.SemaphoreType.DMA
    held = pl.BlockSpec(memory_space=pltpu.VMEM)
    left = pl.BlockSpec(memory_space=pl.ANY)
    exchange = pltpu.VMEM((devices, rows, cols), jnp.bfloat16)
    return pl.pallas_call(
        layer_kernel,
        name="layer",
        out_shape=jax.ShapeDtypeStruct((rows, cols), jnp.bfloat16),
        in_specs=[held, held, left, left, held, left, left, left, left, held],
        out_specs=held,
        scratch_shapes=[
            pltpu.VMEM(q_weight.shape, jnp.bfloat16),
            pltpu.VMEM(o_weight.shape, jnp.bfloat16),
            pltpu.VMEM(gate_weight.shape, jnp.bfloat16),
            pltpu.VMEM(up_weight.shape, jnp.bfloat16),
            pltpu.VMEM(down_weight.shape, jnp.bfloat16),
            exchange,
            exchange,
            exchange,
            pltpu.VMEM((rows, cols), jnp.bfloat16),
            pltpu.VMEM((devices, 2, BLOCK, HEAD_DIM), jnp.bfloat16),
            pltpu.VMEM((KV_HEADS, rows, HEAD_DIM), jnp.float32),
            pltpu.VMEM((devices, rows, HEAD_DIM), jnp.float32),
            pltpu.VMEM((devices, rows * cols // HEAD_DIM, BLOCK), jnp.float32),
            exchange,
            exchange,
            exchange,
            exchange,
            pltpu.VMEM((rows, cols), jnp.float32),
            dma((5,)),
            dma(()),
            *([dma((chips,)), dma((devices,)), dma((chips,))] * 4),
            *([dma((devices,))] * 4),
        ],
        compiler_params=pltpu.CompilerParams(
            collective_id=0, has_side_effects=True, vmem_limit_bytes=67043328
        ),
    )(
        x_rows,
        attn_gain,
        q_weight,
        o_weight,
        mlp_gain,
        gate_weight,
        up_weight,
        down_weight,
        kv_cache,
        block_mask[:, :, 0],
    )


def solution(mesh):
    fused = mesh.shape["seq"] == 2 * KV_HEADS
    return jax.shard_map(
        layer if fused else local,
        mesh=mesh,
        in_specs=(
            P("group", "seq"),
            P(),
            P(None, "seq"),
            P("seq", None),
            P(),
            P(None, "seq"),
            P(None, "seq"),
            P("seq", None),
            P(None, ("group", "seq"), None),
            P("group", None, "seq"),
        ),
        out_specs=P("group", "seq"),
        check_vma=False,
    )
```

profile of v0, /device:TPU:0, one launch (start us, length us, event | category | flops | bytes accessed | tf_op | source)
XLA Modules:
  0.0 57.6 jit_solution(1115243820792359809)
XLA Ops:
  0.0 1.4 %copy.11.mask_ref = s32[16,8]{1,0:T(8,128)} copy(s32[16,8]{0,1:T(8,128)} %bitcast.1) | data formatting | bytes 1024 | tf_op jit(solution)/shard_map/squeeze | solution.py:495
  1.4 54.9 %layer.1 = bf16[16,512]{1,0:T(8,128)(2,1)} custom-call(bf16[16,512]{1,0:T(8,128)(2,1)} %x_ref.1, bf16[8192]{0:T(1024)(128)(2,1)} %attn_gain.1, bf16[8192,512]{1,0:T(8,128)(2,1)} %q_hbm.1, bf16[512,8192]{1,0:T(8,128)(2,1)} %o_hbm.1, bf16[8192]{0:T(1024)(128)(2,1)} %mlp_gain.1, bf16[8192,896]{1,0:T(8,128)(2,1)} %gate_hbm.1, bf16[8192,896]{1,0:T(8,128)(2,1)} %up_hbm.1, ...), custom_call_target="tpu_custom_call" | custom-call | tf_op jit(solution)/shard_map/layer/pallas_call | solution.py:452
  56.3 1.3 %copy.13 = bf16[16,512]{1,0:T(8,128)(2,1)} copy(bf16[16,512]{1,0:T(8,128)(2,1)} %layer.1) | data formatting | bytes 32768
where the time goes:
time: 58 us; the launch traced here: 57.6 us
  Pallas kernels  54.9 us (95%)
  local copies, waits for them, and re-layouts  2.68 us (5%)
    pallas_call x1, Pallas kernels, layer(): pl.pallas_call(layer_kernel, name='layer', out_shape=jax.ShapeDtypeStruct...  54.9 us
    squeeze x1, local copies, waits for them, and re-layouts, layer(): block_mask[:, :, 0]  1.35 us
    unnamed x1, local copies, waits for them, and re-layouts  1.32 us

commit v1 on v0

v1 whole, which is shorter than its diff:
```python
import functools

import jax
import jax.numpy as jnp
from jax import lax
from jax.experimental import pallas as pl
from jax.experimental.pallas import tpu as pltpu
from jax.sharding import PartitionSpec as P

HEADS = 64
KV_HEADS = 8
HEAD_DIM = 128
BLOCK = 128


eps = 1e-05
floor_score = -1e30


def combined_all(x, axis, combine):
    everything = jax.tree.map(lambda part: lax.all_gather(part, axis), x)
    initial = jax.tree.map(lambda part: part[0], everything)

    def turn(k, so_far):
        return combine(so_far, jax.tree.map(lambda part: part[k], everything))

    return lax.fori_loop(1, lax.axis_size(axis), turn, initial)


def rms_norm(values, gain):
    wide = values.astype(jnp.float32)
    inverse = lax.rsqrt(jnp.mean(wide * wide, axis=-1, keepdims=True) + eps)
    return (wide * inverse * gain.astype(jnp.float32)).astype(jnp.bfloat16)


def combine_states(first, second):
    top_a, total_a, accum_a = first
    top_b, total_b, accum_b = second
    top = jnp.maximum(top_a, top_b)
    factor_a = jnp.exp(top_a - top)
    factor_b = jnp.exp(top_b - top)
    return (
        top,
        total_a * factor_a + total_b * factor_b,
        accum_a * factor_a[..., None] + accum_b * factor_b[..., None],
    )


def local(
    x_rows,
    attn_gain,
    q_weight,
    o_weight,
    mlp_gain,
    gate_weight,
    up_weight,
    down_weight,
    kv_cache,
    block_mask,
):
    rows = x_rows.shape[0]
    group = HEADS // KV_HEADS
    key_len = kv_cache.shape[1]
    spans = key_len // BLOCK
    scale = 1.0 / HEAD_DIM**0.5
    whole = lax.all_gather(x_rows, "seq", axis=1, tiled=True)
    normed = rms_norm(whole, attn_gain)
    query_part = jnp.dot(normed, q_weight, preferred_element_type=jnp.float32).astype(jnp.bfloat16)
    queries = lax.all_gather(query_part, "seq", axis=1, tiled=True)
    doc_keys = kv_cache[0]
    doc_values = kv_cache[1]

    def one_group(index):
        query_group = lax.dynamic_slice_in_dim(
            queries, index * (group * HEAD_DIM), group * HEAD_DIM, 1
        ).reshape(rows, group, HEAD_DIM)
        key_group = lax.dynamic_slice_in_dim(doc_keys, index * HEAD_DIM, HEAD_DIM, 1)
        value_group = lax.dynamic_slice_in_dim(doc_values, index * HEAD_DIM, HEAD_DIM, 1)
        mask_group = lax.dynamic_slice_in_dim(block_mask, index, 1, 1)[:, 0, :]
        scores = (
            jnp.einsum("rhd,kd->rhk", query_group, key_group, preferred_element_type=jnp.float32)
            * scale
        )
        scores = scores.reshape(rows, group, spans, BLOCK)
        live = (mask_group == 1)[:, None, :, None]
        masked = jnp.where(live, scores, floor_score)
        local_top = jnp.max(masked, axis=(2, 3))
        weights = jnp.where(live, jnp.exp(masked - local_top[..., None, None]), 0.0)
        local_total = jnp.sum(weights, axis=(2, 3))
        rounded = weights.astype(jnp.bfloat16).reshape(rows, group, key_len)
        local_accum = jnp.einsum(
            "rhk,kd->rhd", rounded, value_group, preferred_element_type=jnp.float32
        )
        return (local_top, local_total, local_accum)

    tops, totals, accums = lax.map(one_group, jnp.arange(KV_HEADS, dtype=jnp.int32))
    local_top = jnp.moveaxis(tops, 0, 1)
    local_total = jnp.moveaxis(totals, 0, 1)
    local_accum = jnp.moveaxis(accums, 0, 1)
    columns = q_weight.shape[1]
    col_start = lax.axis_index("seq") * columns
    top, total, accum = combined_all((local_top, local_total, local_accum), "seq", combine_states)
    attended = accum / total[..., None]
    attended = attended.reshape(rows, HEADS * HEAD_DIM).astype(jnp.bfloat16)
    attn_cols = lax.dynamic_slice_in_dim(attended, col_start, columns, 1)
    weight_cols = o_weight
    attn_out = lax.psum_scatter(
        lax.dot_general(
            weight_cols, attn_cols, (((0,), (1,)), ((), ())), preferred_element_type=jnp.float32
        ),
        "seq",
        scatter_dimension=0,
        tiled=True,
    )
    stream = (x_rows.astype(jnp.float32) + attn_out.T).astype(jnp.bfloat16)
    stream_whole = lax.all_gather(stream, "seq", axis=1, tiled=True)
    normed_two = rms_norm(stream_whole, mlp_gain)
    gate = jnp.dot(normed_two, gate_weight, preferred_element_type=jnp.float32)
    upward = jnp.dot(normed_two, up_weight, preferred_element_type=jnp.float32)
    hidden = (jax.nn.silu(gate) * upward).astype(jnp.bfloat16)
    weight_cols = down_weight
    down_out = lax.psum_scatter(
        lax.dot_general(
            weight_cols, hidden, (((0,), (1,)), ((), ())), preferred_element_type=jnp.float32
        ),
        "seq",
        scatter_dimension=0,
        tiled=True,
    )
    return (stream.astype(jnp.float32) + down_out.T).astype(jnp.bfloat16)


SCALE = 1.0 / HEAD_DIM**0.5
MASK_AT = 2 * BLOCK


def layer_kernel(
    x_hbm,
    gain_one_hbm,
    q_hbm,
    o_hbm,
    gain_two_hbm,
    gate_hbm,
    up_hbm,
    down_hbm,
    kv_hbm,
    mask_hbm,
    y_ref,
    q_w,
    o_w,
    gate_w,
    up_w,
    down_w,
    gain_one,
    gain_two,
    mask_ref,
    x_all,
    s_all,
    normed,
    kv_stage,
    kv_all,
    scores,
    q_own,
    q_got,
    piece,
    piece_got,
    duo_one,
    duo_got_one,
    part_one,
    got_one,
    duo_two,
    duo_got_two,
    part_two,
    got_two,
    own_ref,
    w_sem,
    in_sem,
    stage_sem,
    kv_own_sem,
    x_send,
    x_recv,
    x_pass,
    s_send,
    s_recv,
    s_pass,
    kv_send,
    kv_recv,
    q_send,
    q_recv,
    piece_send,
    piece_recv,
    duo_send_one,
    duo_recv_one,
    send_one,
    recv_one,
    duo_send_two,
    duo_recv_two,
    send_two,
    recv_two,
):
    devices, rows, cols = x_all.shape
    chips = devices // 2
    near = chips // 2
    group = cols // HEAD_DIM
    lines = group * rows
    me = lax.axis_index("seq")
    chip = me // 2
    core = me % 2
    partner = chip * 2 + 1 - core
    half = chip // near
    spot = chip % near
    mirror = (chip + near) % chips
    lane = me % chips

    def remote(src, dst, send, recv, device):
        return pltpu.make_async_remote_copy(
            src_ref=src,
            dst_ref=dst,
            send_sem=send,
            recv_sem=recv,
            device_id={"seq": device},
            device_id_type=pl.DeviceIdType.MESH,
        )

    def step_off(s):
        return chips // 2 + ((s + 1) // 2) * (1 - 2 * (s % 2))

    far_first = [step_off(s) for s in range(chips - 1)]

    def chip_at(off):
        return (chip + off) % chips

    barrier = pltpu.get_barrier_semaphore()
    for off in range(1, devices):
        pl.semaphore_signal(
            barrier,
            inc=1,
            device_id={"seq": (me + off) % devices},
            device_id_type=pl.DeviceIdType.MESH,
        )

    load_x = pltpu.make_async_copy(x_hbm, x_all.at[me], in_sem.at[0])
    load_mask = pltpu.make_async_copy(mask_hbm, mask_ref, in_sem.at[1])
    load_gain_one = pltpu.make_async_copy(gain_one_hbm, gain_one, in_sem.at[2])
    load_gain_two = pltpu.make_async_copy(gain_two_hbm, gain_two, in_sem.at[3])
    load_x.start()
    load_mask.start()
    stages = []
    for g in range(KV_HEADS):
        for side in range(2):
            stages.append(
                pltpu.make_async_copy(
                    kv_hbm.at[side, :, pl.ds(g * HEAD_DIM, HEAD_DIM)],
                    kv_stage.at[g // near, g % near, pl.ds(side * BLOCK, BLOCK)],
                    stage_sem.at[2 * g + side],
                )
            )
            stages[-1].start()
    load_gain_one.start()
    load_gain_two.start()

    def fetch(k, src, dst):
        return pltpu.make_async_copy(src, dst, w_sem.at[k])

    fetch_q = fetch(0, q_hbm, q_w)
    fetch_o = fetch(1, o_hbm, o_w)
    fetch_gate = fetch(2, gate_hbm, gate_w)
    fetch_up = fetch(3, up_hbm, up_w)
    fetch_down = fetch(4, down_hbm, down_w)
    fetch_q.start()
    fetch_o.start()

    load_mask.wait()
    across = lax.broadcasted_iota(jnp.int32, (rows, rows), 1)
    down = lax.broadcasted_iota(jnp.int32, (rows, rows), 0)
    for g in range(KV_HEADS):
        flat = jnp.broadcast_to(mask_ref[g].astype(jnp.float32), (rows, rows))
        column = jnp.sum(jnp.where(across == down, flat, 0.0), axis=1, keepdims=True)
        kv_stage[g // near, g % near, pl.ds(MASK_AT, rows), :] = jnp.broadcast_to(
            column, (rows, HEAD_DIM)
        ).astype(jnp.bfloat16)
    load_x.wait()
    for stage in stages:
        stage.wait()
    own_kv = pltpu.make_async_copy(kv_stage.at[core, spot], kv_all.at[lane], kv_own_sem)
    own_kv.start()
    with jax.named_scope("t_barrier"):
        pl.semaphore_wait(barrier, devices - 1)

    def gather_start(dst, send, recv):
        for off in far_first:
            remote(
                dst.at[me], dst.at[me], send.at[off], recv.at[me], chip_at(off) * 2 + core
            ).start()
        remote(dst.at[me], dst.at[me], send.at[0], recv.at[me], partner).start()

    def gather_pass(dst, send, recv, hand):
        for off in reversed(far_first):
            other = chip_at(off) * 2 + core
            remote(dst.at[other], dst.at[other], send.at[off], recv.at[other], partner).wait_recv()
            remote(dst.at[other], dst.at[other], hand.at[off], recv.at[other], partner).start()

    def gather_finish(dst, send, recv):
        for off in range(chips):
            other = chip_at(off) * 2 + 1 - core
            remote(dst.at[other], dst.at[other], send.at[0], recv.at[other], partner).wait_recv()

    def gather_drain(dst, send, recv, hand):
        for off in range(chips):
            remote(dst.at[me], dst.at[me], send.at[off], recv.at[me], partner).wait_send()
        for off in far_first:
            remote(dst.at[me], dst.at[me], hand.at[off], recv.at[me], partner).wait_send()

    gather_start(x_all, x_send, x_recv)

    for k in range(chips - 1, 0, -1):
        there = (spot + k // 2) % near
        side = (core + k) % 2
        remote(
            kv_stage.at[side, there],
            kv_all.at[lane],
            kv_send.at[k],
            kv_recv.at[lane],
            (half * near + there) * 2 + side,
        ).start()
    fetch_gate.start()
    fetch_up.start()
    fetch_down.start()

    def norm(values, gain):
        squares = jnp.zeros((rows, cols), jnp.float32)
        for i in range(devices):
            wide = values[i].astype(jnp.float32)
            squares = squares + wide * wide
        mean = jnp.sum(squares, axis=-1, keepdims=True) * (1.0 / (devices * cols))
        inverse = lax.rsqrt(mean + eps)
        for i in range(devices):
            part_gain = gain[i * cols : (i + 1) * cols].astype(jnp.float32).reshape(1, cols)
            normed[i] = (values[i].astype(jnp.float32) * inverse * part_gain).astype(jnp.bfloat16)

    with jax.named_scope("t_xgather"):
        gather_pass(x_all, x_send, x_recv, x_pass)
        load_gain_one.wait()
        load_gain_two.wait()
        gather_finish(x_all, x_send, x_recv)
    norm(x_all, gain_one)
    with jax.named_scope("t_fetchq"):
        fetch_q.wait()
    step = 4

    def q_step(t, total):
        for u in range(step):
            i = t * step + u
            total = total + jnp.dot(
                normed[i],
                q_w[pl.ds(pl.multiple_of(i * cols, cols), cols), :],
                preferred_element_type=jnp.float32,
            )
        return total

    with jax.named_scope("t_qmm"):
        queries = lax.fori_loop(
            0, devices // step, q_step, jnp.zeros((rows, cols), jnp.float32)
        ).astype(jnp.bfloat16)
        q_own[...] = jnp.concatenate(
            [queries[:, h * HEAD_DIM : (h + 1) * HEAD_DIM] for h in range(group)], axis=0
        )

    keeps = core == half
    to_mirror = remote(
        q_own, q_got.at[core], q_send.at[0], q_recv.at[core], mirror * 2 + half
    )
    to_partner = remote(q_own, q_got.at[core], q_send.at[1], q_recv.at[core], partner)
    to_mirror.start()

    @pl.when(jnp.logical_not(keeps))
    def _():
        to_partner.start()

    @pl.when(keeps)
    def _():
        q_got[core] = q_own[...]

    with jax.named_scope("t_kvwait"):
        own_kv.wait()
        for c in range(1, chips):
            other = (lane + c) % chips
            remote(
                kv_all.at[other], kv_all.at[other], kv_send.at[0], kv_recv.at[other], partner
            ).wait_recv()

    def q_arrived(which):
        remote(q_own, q_got.at[which], q_send.at[0], q_recv.at[which], partner).wait_recv()

    with jax.named_scope("t_qwait"):
        q_arrived(1 - core)

        @pl.when(jnp.logical_not(keeps))
        def _():
            q_arrived(core)

    tops = []
    with jax.named_scope("t_attn"):
        query = jnp.concatenate([q_got[0], q_got[1]], axis=0)

        def live_at(c):
            mask = kv_all[c, pl.ds(MASK_AT, rows), :].astype(jnp.float32)
            return jnp.concatenate([mask] * (2 * group), axis=0) > 0.5

        for c in range(chips):
            score = (
                lax.dot_general(
                    query,
                    kv_all[c, pl.ds(0, BLOCK), :],
                    (((1,), (1,)), ((), ())),
                    preferred_element_type=jnp.float32,
                )
                * SCALE
            )
            masked = jnp.where(live_at(c), score, floor_score)
            scores[c] = masked
            tops.append(jnp.max(masked, axis=-1, keepdims=True))
        top = functools.reduce(jnp.maximum, tops)
        total = jnp.zeros((2 * lines, 1), jnp.float32)
        accum = jnp.zeros((2 * lines, HEAD_DIM), jnp.float32)
        for c in range(chips):
            weight = jnp.where(live_at(c), jnp.exp(scores[c] - tops[c]), 0.0)
            factor = jnp.exp(tops[c] - top)
            total = total + factor * jnp.sum(weight, axis=-1, keepdims=True)
            accum = accum + factor * jnp.dot(
                weight.astype(jnp.bfloat16),
                kv_all[c, pl.ds(BLOCK, BLOCK), :],
                preferred_element_type=jnp.float32,
            )
        row = lax.broadcasted_iota(jnp.int32, (lines, HEAD_DIM), 0)
        column = lax.broadcasted_iota(jnp.int32, (lines, HEAD_DIM), 1)
        for s in range(2):
            at = slice(s * lines, (s + 1) * lines)
            spread = jnp.where(
                column == row, top[at], jnp.where(column == row + lines, total[at], 0.0)
            )
            piece[s, pl.ds(0, lines), :] = accum[at]
            piece[s, pl.ds(lines, 8), :] = jnp.broadcast_to(
                jnp.sum(spread, axis=0, keepdims=True), (8, HEAD_DIM)
            )

    def piece_copy(which, slot, device):
        return remote(
            piece.at[which], piece_got.at[slot], piece_send.at[which], piece_recv.at[slot], device
        )

    @pl.when(keeps)
    def _():
        piece_copy(1 - core, 0, partner).start()
        piece_got[0] = piece[core]

    @pl.when(jnp.logical_not(keeps))
    def _():
        piece_copy(0, 1, mirror * 2).start()
        piece_copy(1, 1, mirror * 2 + 1).start()

    with jax.named_scope("t_piece"):

        @pl.when(jnp.logical_not(keeps))
        def _():
            piece_copy(0, 0, partner).wait_recv()

        piece_copy(0, 1, partner).wait_recv()

    with jax.named_scope("t_join"):

        def parts_of(slot):
            stats = jnp.broadcast_to(piece_got[slot, pl.ds(lines, 1), :], (lines, HEAD_DIM))
            high = jnp.sum(jnp.where(column == row, stats, 0.0), axis=1, keepdims=True)
            mass = jnp.sum(jnp.where(column == row + lines, stats, 0.0), axis=1, keepdims=True)
            return high, mass, piece_got[slot, pl.ds(0, lines), :]

        top_a, total_a, accum_a = parts_of(0)
        top_b, total_b, accum_b = parts_of(1)
        high = jnp.maximum(top_a, top_b)
        factor_a = jnp.exp(top_a - high)
        factor_b = jnp.exp(top_b - high)
        ratio = (accum_a * factor_a + accum_b * factor_b) / (
            total_a * factor_a + total_b * factor_b
        )
        attended = jnp.concatenate(
            [ratio[h * rows : (h + 1) * rows] for h in range(group)], axis=1
        ).astype(jnp.bfloat16)

    def scatter(values, weight, duo, duo_got, duo_send, duo_recv, part, got, send, recv):
        def product(to):
            return jnp.dot(
                values,
                weight[:, pl.ds(pl.multiple_of(to * cols, cols), cols)],
                preferred_element_type=jnp.float32,
            )

        def give(s):
            return remote(duo.at[s], duo_got.at[s], duo_send.at[s], duo_recv.at[s], partner)

        def post(s):
            return remote(
                part.at[s],
                got.at[chip],
                send.at[s],
                recv.at[chip],
                chip_at(step_off(s)) * 2 + core,
            )

        def turn_one(t, _):
            first = product(chip_at(step_off(2 * t)) * 2 + 1 - core)
            second = product(chip_at(step_off(2 * t + 1)) * 2 + 1 - core)
            duo[2 * t] = first
            duo[2 * t + 1] = second

            @pl.when(t > 0)
            def _():
                give(2 * t - 2).start()
                give(2 * t - 1).start()

            return 0

        def turn_two(t, _):
            first = product(chip_at(step_off(2 * t)) * 2 + core)
            second = product(chip_at(step_off(2 * t + 1)) * 2 + core)
            give(2 * t).wait_recv()
            give(2 * t + 1).wait_recv()
            first = first + duo_got[2 * t]
            second = second + duo_got[2 * t + 1]
            part[2 * t] = first.astype(part.dtype)
            part[2 * t + 1] = second.astype(part.dtype)
            own_ref[...] = second

            @pl.when(t > 0)
            def _():
                post(2 * t - 2).start()
                post(2 * t - 1).start()

            return 0

        with jax.named_scope("t_prod1"):
            lax.fori_loop(0, chips // 2, turn_one, 0)
            give(chips - 2).start()
            give(chips - 1).start()
        with jax.named_scope("t_prod2"):
            lax.fori_loop(0, chips // 2, turn_two, 0)
            post(chips - 2).start()

        total = own_ref[...]
        for s in range(chips - 2, -1, -1):
            other = chip_at(step_off(s))
            remote(
                part.at[s], got.at[other], send.at[s], recv.at[other], other * 2 + core
            ).wait_recv()
            total = total + got[other].astype(jnp.float32)
        return total

    def scatter_drain(duo, duo_got, duo_send, duo_recv, part, got, send, recv):
        for s in range(chips):
            remote(duo.at[s], duo_got.at[s], duo_send.at[s], duo_recv.at[s], partner).wait_send()
        for s in range(chips - 1):
            remote(part.at[s], got.at[chip], send.at[s], recv.at[chip], partner).wait_send()

    one = (duo_one, duo_got_one, duo_send_one, duo_recv_one, part_one, got_one, send_one, recv_one)
    two = (duo_two, duo_got_two, duo_send_two, duo_recv_two, part_two, got_two, send_two, recv_two)
    with jax.named_scope("t_fetcho"):
        fetch_o.wait()
    with jax.named_scope("t_scat1"):
        attn_out = scatter(attended, o_w, *one)
    stream = (x_all[me].astype(jnp.float32) + attn_out).astype(jnp.bfloat16)
    s_all[me] = stream
    gather_start(s_all, s_send, s_recv)
    with jax.named_scope("t_sgather"):
        gather_pass(s_all, s_send, s_recv, s_pass)
        gather_finish(s_all, s_send, s_recv)
    norm(s_all, gain_two)
    with jax.named_scope("t_fetchgu"):
        fetch_gate.wait()
        fetch_up.wait()
    wide = gate_w.shape[1]

    def ff_step(t, sums):
        gate, upward = sums
        for u in range(2):
            i = t * 2 + u
            at = pl.ds(pl.multiple_of(i * cols, cols), cols)
            gate = gate + jnp.dot(normed[i], gate_w[at, :], preferred_element_type=jnp.float32)
            upward = upward + jnp.dot(normed[i], up_w[at, :], preferred_element_type=jnp.float32)
        return gate, upward

    zeros = jnp.zeros((rows, wide), jnp.float32)
    with jax.named_scope("t_ffmm"):
        gate, upward = lax.fori_loop(0, devices // 2, ff_step, (zeros, zeros))
    hidden = (gate / (1.0 + jnp.exp(-gate)) * upward).astype(jnp.bfloat16)
    with jax.named_scope("t_fetchd"):
        fetch_down.wait()
    with jax.named_scope("t_scat2"):
        down_out = scatter(hidden, down_w, *two)
    y_ref[...] = (s_all[me].astype(jnp.float32) + down_out).astype(jnp.bfloat16)

    with jax.named_scope("t_drain"):
        gather_drain(x_all, x_send, x_recv, x_pass)
        gather_drain(s_all, s_send, s_recv, s_pass)
        for k in range(1, chips):
            remote(
                kv_stage.at[0, 0], kv_all.at[lane], kv_send.at[k], kv_recv.at[lane], partner
            ).wait_send()
        to_mirror.wait_send()

        @pl.when(jnp.logical_not(keeps))
        def _():
            to_partner.wait_send()
            piece_copy(0, 1, partner).wait_send()
            piece_copy(1, 1, partner).wait_send()

        @pl.when(keeps)
        def _():
            piece_copy(1 - core, 0, partner).wait_send()

        scatter_drain(*one)
        scatter_drain(*two)


def layer(
    x_rows,
    attn_gain,
    q_weight,
    o_weight,
    mlp_gain,
    gate_weight,
    up_weight,
    down_weight,
    kv_cache,
    block_mask,
):
    rows, cols = x_rows.shape
    devices = lax.axis_size("seq")
    chips = devices // 2
    lines = rows * cols // HEAD_DIM
    dma = pltpu.SemaphoreType.DMA
    left = pl.BlockSpec(memory_space=pl.ANY)
    exchange = pltpu.VMEM((devices, rows, cols), jnp.bfloat16)
    duo = pltpu.VMEM((chips, rows, cols), jnp.float32)
    part = pltpu.VMEM((chips, rows, cols), jnp.bfloat16)
    pieces = pltpu.VMEM((2, lines + 8, HEAD_DIM), jnp.float32)
    return pl.pallas_call(
        layer_kernel,
        name="layer",
        out_shape=jax.ShapeDtypeStruct((rows, cols), jnp.bfloat16),
        in_specs=[left] * 10,
        out_specs=pl.BlockSpec(memory_space=pltpu.VMEM),
        scratch_shapes=[
            pltpu.VMEM(q_weight.shape, jnp.bfloat16),
            pltpu.VMEM(o_weight.shape, jnp.bfloat16),
            pltpu.VMEM(gate_weight.shape, jnp.bfloat16),
            pltpu.VMEM(up_weight.shape, jnp.bfloat16),
            pltpu.VMEM(down_weight.shape, jnp.bfloat16),
            pltpu.VMEM(attn_gain.shape, jnp.bfloat16),
            pltpu.VMEM(mlp_gain.shape, jnp.bfloat16),
            pltpu.VMEM((KV_HEADS, 1, rows), jnp.int32),
            exchange,
            exchange,
            exchange,
            pltpu.VMEM((2, chips // 2, MASK_AT + rows, HEAD_DIM), jnp.bfloat16),
            pltpu.VMEM((chips, MASK_AT + rows, HEAD_DIM), jnp.bfloat16),
            pltpu.VMEM((chips, 2 * lines, BLOCK), jnp.float32),
            pltpu.VMEM((lines, HEAD_DIM), jnp.bfloat16),
            pltpu.VMEM((2, lines, HEAD_DIM), jnp.bfloat16),
            pieces,
            pieces,
            *([duo, duo, part, part] * 2),
            pltpu.VMEM((rows, cols), jnp.float32),
            dma((5,)),
            dma((4,)),
            dma((2 * KV_HEADS,)),
            dma(()),
            *([dma((chips,)), dma((devices,)), dma((chips,))] * 2),
            dma((chips,)),
            dma((chips,)),
            *([dma((2,))] * 4),
            *([dma((chips,))] * 8),
        ],
        compiler_params=pltpu.CompilerParams(
            collective_id=0, has_side_effects=True, vmem_limit_bytes=67043328
        ),
    )(
        x_rows,
        attn_gain,
        q_weight,
        o_weight,
        mlp_gain,
        gate_weight,
        up_weight,
        down_weight,
        kv_cache,
        jnp.transpose(block_mask, (1, 2, 0)),
    )


def solution(mesh):
    fused = mesh.shape["seq"] == 2 * KV_HEADS
    return jax.shard_map(
        layer if fused else local,
        mesh=mesh,
        in_specs=(
            P("group", "seq"),
            P(),
            P(None, "seq"),
            P("seq", None),
            P(),
            P(None, "seq"),
            P(None, "seq"),
            P("seq", None),
            P(None, ("group", "seq"), None),
            P("group", None, "seq"),
        ),
        out_specs=P("group", "seq"),
        check_vma=False,
    )
```

time: 58 us -> 52.5 us (0.905)
  Pallas kernels: 54.9 us -> 50.9 us
  local copies, waits for them, and re-layouts: 2.68 us -> 1.32 us
    pallas_call x1, Pallas kernels: 54.9 us -> 50.9 us  [layer(): pl.pallas_call(layer_kernel, name='layer', out_shape=jax.ShapeDtypeStruct...]
    squeeze x1 -> x0, local copies, waits for them, and re-layouts: 1.35 us -> none  [layer(): block_mask[:, :, 0]]
where the time goes in v1:
time: 52.5 us; the launch traced here: 52.2 us
  Pallas kernels  50.9 us (97%)
  local copies, waits for them, and re-layouts  1.32 us (3%)
    pallas_call x1, Pallas kernels, layer(): pl.pallas_call(layer_kernel, name='layer', out_shape=jax.ShapeDtypeStruct...  50.9 us
    unnamed x1, local copies, waits for them, and re-layouts  1.32 us

profile of v1, /device:TPU:0, one launch (start us, length us, event | category | flops | bytes accessed | tf_op | source)
XLA Modules:
  0.0 52.2 jit_solution(11562755198659936649)
XLA Ops:
  0.0 50.9 %layer.1 = bf16[16,512]{1,0:T(8,128)(2,1)} custom-call(bf16[16,512]{1,0:T(8,128)(2,1)} %x_hbm.1, bf16[8192]{0:T(1024)(128)(2,1)} %gain_one_hbm.1, bf16[8192,512]{1,0:T(8,128)(2,1)} %q_hbm.1, bf16[512,8192]{1,0:T(8,128)(2,1)} %o_hbm.1, bf16[8192]{0:T(1024)(128)(2,1)} %gain_two_hbm.1, bf16[8192,896]{1,0:T(8,128)(2,1)} %gate_hbm.1, bf16[8192,896]{1,0:T(8,128)(2,1)} %up_hbm.1, ...), custom_call_target="tpu_custom_call" | custom-call | tf_op jit(solution)/shard_map/layer/pallas_call | solution.py:646
  50.9 1.3 %copy.12 = bf16[16,512]{1,0:T(8,128)(2,1)} copy(bf16[16,512]{1,0:T(8,128)(2,1)} %layer.1) | data formatting | bytes 32768

commit v2 on v1

--- a/solution.py
+++ b/solution.py
@@ -178,11 +178,11 @@
     stage_sem,
     kv_own_sem,
     x_send,
-    x_recv,
-    x_pass,
+    x_near,
+    x_far,
     s_send,
-    s_recv,
-    s_pass,
+    s_near,
+    s_far,
     kv_send,
     kv_recv,
     q_send,
@@ -222,13 +222,15 @@
             device_id_type=pl.DeviceIdType.MESH,
         )
 
-    def step_off(s):
-        return chips // 2 + ((s + 1) // 2) * (1 - 2 * (s % 2))
-
-    far_first = [step_off(s) for s in range(chips - 1)]
-
-    def chip_at(off):
-        return (chip + off) % chips
+    def chip_at(way):
+        return sum(
+            ((chip // bit + way // bit) % 2) * bit for bit in (1, 2, 4)
+        )
+
+    far_first = list(range(chips - 1, 0, -1))
+
+    def whole(ref, sem):
+        return pltpu.make_async_copy(ref, ref, sem)
 
     barrier = pltpu.get_barrier_semaphore()
     for off in range(1, devices):
@@ -252,7 +254,7 @@
                 pltpu.make_async_copy(
                     kv_hbm.at[side, :, pl.ds(g * HEAD_DIM, HEAD_DIM)],
                     kv_stage.at[g // near, g % near, pl.ds(side * BLOCK, BLOCK)],
-                    stage_sem.at[2 * g + side],
+                    stage_sem,
                 )
             )
             stages[-1].start()
@@ -269,6 +271,33 @@
     fetch_down = fetch(4, down_hbm, down_w)
     fetch_q.start()
     fetch_o.start()
+
+    load_x.wait()
+    with jax.named_scope("t_barrier"):
+        pl.semaphore_wait(barrier, devices - 1)
+
+    def gather_start(dst, send, near_recv, far_recv):
+        for way in far_first:
+            remote(
+                dst.at[me], dst.at[me], send, far_recv.at[way], chip_at(way) * 2 + core
+            ).start()
+        remote(dst.at[me], dst.at[me], send, near_recv, partner).start()
+
+    def gather_pass(dst, send, near_recv, far_recv):
+        for way in reversed(far_first):
+            other = chip_at(way) * 2 + core
+            remote(dst.at[other], dst.at[other], send, far_recv.at[way], partner).wait_recv()
+            remote(dst.at[other], dst.at[other], send, near_recv, partner).start()
+
+    def gather_finish(dst, send, near_recv, far_recv):
+        whole(dst.at[pl.ds(0, chips)], near_recv).wait()
+
+    def gather_drain(dst, send, near_recv, far_recv):
+        whole(dst.at[pl.ds(0, devices - 1)], send).wait()
+
+    x_sems = (x_all, x_send, x_near, x_far)
+    s_sems = (s_all, s_send, s_near, s_far)
+    gather_start(*x_sems)
 
     load_mask.wait()
     across = lax.broadcasted_iota(jnp.int32, (rows, rows), 1)
@@ -279,49 +308,20 @@
         kv_stage[g // near, g % near, pl.ds(MASK_AT, rows), :] = jnp.broadcast_to(
             column, (rows, HEAD_DIM)
         ).astype(jnp.bfloat16)
-    load_x.wait()
-    for stage in stages:
-        stage.wait()
+    with jax.named_scope("t_stage"):
+        whole(kv_stage.at[:, :, pl.ds(0, MASK_AT)], stage_sem).wait()
     own_kv = pltpu.make_async_copy(kv_stage.at[core, spot], kv_all.at[lane], kv_own_sem)
     own_kv.start()
-    with jax.named_scope("t_barrier"):
-        pl.semaphore_wait(barrier, devices - 1)
-
-    def gather_start(dst, send, recv):
-        for off in far_first:
-            remote(
-                dst.at[me], dst.at[me], send.at[off], recv.at[me], chip_at(off) * 2 + core
-            ).start()
-        remote(dst.at[me], dst.at[me], send.at[0], recv.at[me], partner).start()
-
-    def gather_pass(dst, send, recv, hand):
-        for off in reversed(far_first):
-            other = chip_at(off) * 2 + core
-            remote(dst.at[other], dst.at[other], send.at[off], recv.at[other], partner).wait_recv()
-            remote(dst.at[other], dst.at[other], hand.at[off], recv.at[other], partner).start()
-
-    def gather_finish(dst, send, recv):
-        for off in range(chips):
-            other = chip_at(off) * 2 + 1 - core
-            remote(dst.at[other], dst.at[other], send.at[0], recv.at[other], partner).wait_recv()
-
-    def gather_drain(dst, send, recv, hand):
-        for off in range(chips):
-            remote(dst.at[me], dst.at[me], send.at[off], recv.at[me], partner).wait_send()
-        for off in far_first:
-            remote(dst.at[me], dst.at[me], hand.at[off], recv.at[me], partner).wait_send()
-
-    gather_start(x_all, x_send, x_recv)
 
     for k in range(chips - 1, 0, -1):
-        there = (spot + k // 2) % near
+        there = chip_at(k // 2)
         side = (core + k) % 2
         remote(
-            kv_stage.at[side, there],
+            kv_stage.at[side, there % near],
             kv_all.at[lane],
-            kv_send.at[k],
-            kv_recv.at[lane],
-            (half * near + there) * 2 + side,
+            kv_send,
+            kv_recv,
+            there * 2 + side,
         ).start()
     fetch_gate.start()
     fetch_up.start()
@@ -339,10 +339,10 @@
             normed[i] = (values[i].astype(jnp.float32) * inverse * part_gain).astype(jnp.bfloat16)
 
     with jax.named_scope("t_xgather"):
-        gather_pass(x_all, x_send, x_recv, x_pass)
+        gather_pass(*x_sems)
         load_gain_one.wait()
         load_gain_two.wait()
-        gather_finish(x_all, x_send, x_recv)
+        gather_finish(*x_sems)
     norm(x_all, gain_one)
     with jax.named_scope("t_fetchq"):
         fetch_q.wait()
@@ -383,11 +383,7 @@
 
     with jax.named_scope("t_kvwait"):
         own_kv.wait()
-        for c in range(1, chips):
-            other = (lane + c) % chips
-            remote(
-                kv_all.at[other], kv_all.at[other], kv_send.at[0], kv_recv.at[other], partner
-            ).wait_recv()
+        whole(kv_all.at[pl.ds(0, chips - 1)], kv_recv).wait()
 
     def q_arrived(which):
         remote(q_own, q_got.at[which], q_send.at[0], q_recv.at[which], partner).wait_recv()
@@ -496,33 +492,37 @@
             )
 
         def give(s):
-            return remote(duo.at[s], duo_got.at[s], duo_send.at[s], duo_recv.at[s], partner)
+            return remote(duo.at[s], duo_got.at[s], duo_send, duo_recv.at[s], partner)
 
         def post(s):
             return remote(
                 part.at[s],
                 got.at[chip],
-                send.at[s],
-                recv.at[chip],
-                chip_at(step_off(s)) * 2 + core,
+                send,
+                recv,
+                chip_at(chips - 1 - s) * 2 + core,
             )
 
         def turn_one(t, _):
-            first = product(chip_at(step_off(2 * t)) * 2 + 1 - core)
-            second = product(chip_at(step_off(2 * t + 1)) * 2 + 1 - core)
-            duo[2 * t] = first
-            duo[2 * t + 1] = second
-
             @pl.when(t > 0)
             def _():
                 give(2 * t - 2).start()
                 give(2 * t - 1).start()
 
+            first = product(chip_at(chips - 1 - 2 * t) * 2 + 1 - core)
+            second = product(chip_at(chips - 2 - 2 * t) * 2 + 1 - core)
+            duo[2 * t] = first
+            duo[2 * t + 1] = second
             return 0
 
         def turn_two(t, _):
-            first = product(chip_at(step_off(2 * t)) * 2 + core)
-            second = product(chip_at(step_off(2 * t + 1)) * 2 + core)
+            @pl.when(t > 0)
+            def _():
+                post(2 * t - 2).start()
+                post(2 * t - 1).start()
+
+            first = product(chip_at(chips - 1 - 2 * t) * 2 + core)
+            second = product(chip_at(chips - 2 - 2 * t) * 2 + core)
             give(2 * t).wait_recv()
             give(2 * t + 1).wait_recv()
             first = first + duo_got[2 * t]
@@ -530,12 +530,6 @@
             part[2 * t] = first.astype(part.dtype)
             part[2 * t + 1] = second.astype(part.dtype)
             own_ref[...] = second
-
-            @pl.when(t > 0)
-            def _():
-                post(2 * t - 2).start()
-                post(2 * t - 1).start()
-
             return 0
 
         with jax.named_scope("t_prod1"):
@@ -546,20 +540,15 @@
             lax.fori_loop(0, chips // 2, turn_two, 0)
             post(chips - 2).start()
 
+        whole(part.at[pl.ds(0, chips - 1)], recv).wait()
         total = own_ref[...]
-        for s in range(chips - 2, -1, -1):
-            other = chip_at(step_off(s))
-            remote(
-                part.at[s], got.at[other], send.at[s], recv.at[other], other * 2 + core
-            ).wait_recv()
-            total = total + got[other].astype(jnp.float32)
+        for way in far_first:
+            total = total + got[chip_at(way)].astype(jnp.float32)
         return total
 
     def scatter_drain(duo, duo_got, duo_send, duo_recv, part, got, send, recv):
-        for s in range(chips):
-            remote(duo.at[s], duo_got.at[s], duo_send.at[s], duo_recv.at[s], partner).wait_send()
-        for s in range(chips - 1):
-            remote(part.at[s], got.at[chip], send.at[s], recv.at[chip], partner).wait_send()
+        whole(duo, duo_send).wait()
+        whole(part.at[pl.ds(0, chips - 1)], send).wait()
 
     one = (duo_one, duo_got_one, duo_send_one, duo_recv_one, part_one, got_one, send_one, recv_one)
     two = (duo_two, duo_got_two, duo_send_two, duo_recv_two, part_two, got_two, send_two, recv_two)
@@ -569,10 +558,10 @@
         attn_out = scatter(attended, o_w, *one)
     stream = (x_all[me].astype(jnp.float32) + attn_out).astype(jnp.bfloat16)
     s_all[me] = stream
-    gather_start(s_all, s_send, s_recv)
+    gather_start(*s_sems)
     with jax.named_scope("t_sgather"):
-        gather_pass(s_all, s_send, s_recv, s_pass)
-        gather_finish(s_all, s_send, s_recv)
+        gather_pass(*s_sems)
+        gather_finish(*s_sems)
     norm(s_all, gain_two)
     with jax.named_scope("t_fetchgu"):
         fetch_gate.wait()
@@ -599,12 +588,9 @@
     y_ref[...] = (s_all[me].astype(jnp.float32) + down_out).astype(jnp.bfloat16)
 
     with jax.named_scope("t_drain"):
-        gather_drain(x_all, x_send, x_recv, x_pass)
-        gather_drain(s_all, s_send, s_recv, s_pass)
-        for k in range(1, chips):
-            remote(
-                kv_stage.at[0, 0], kv_all.at[lane], kv_send.at[k], kv_recv.at[lane], partner
-            ).wait_send()
+        gather_drain(*x_sems)
+        gather_drain(*s_sems)
+        whole(kv_all.at[pl.ds(0, chips - 1)], kv_send).wait()
         to_mirror.wait_send()
 
         @pl.when(jnp.logical_not(keeps))
@@ -672,13 +658,13 @@
             pltpu.VMEM((rows, cols), jnp.float32),
             dma((5,)),
             dma((4,)),
-            dma((2 * KV_HEADS,)),
             dma(()),
-            *([dma((chips,)), dma((devices,)), dma((chips,))] * 2),
-            dma((chips,)),
-            dma((chips,)),
+            dma(()),
+            *([dma(()), dma(()), dma((chips,))] * 2),
+            dma(()),
+            dma(()),
             *([dma((2,))] * 4),
-            *([dma((chips,))] * 8),
+            *([dma(()), dma((chips,)), dma(()), dma(())] * 2),
         ],
         compiler_params=pltpu.CompilerParams(
             collective_id=0, has_side_effects=True, vmem_limit_bytes=67043328

time: 52.5 us -> 47.3 us (0.901)
  Pallas kernels: 50.9 us -> 45.7 us
    pallas_call x1, Pallas kernels: 50.9 us -> 45.7 us  [layer(): pl.pallas_call(layer_kernel, name='layer', out_shape=jax.ShapeDtypeStruct...]
where the time goes in v2:
time: 47.3 us; the launch traced here: 47 us
  Pallas kernels  45.7 us (97%)
  local copies, waits for them, and re-layouts  1.32 us (3%)
    pallas_call x1, Pallas kernels, layer(): pl.pallas_call(layer_kernel, name='layer', out_shape=jax.ShapeDtypeStruct...  45.7 us
    unnamed x1, local copies, waits for them, and re-layouts  1.32 us

profile of v2, /device:TPU:0, one launch (start us, length us, event | category | flops | bytes accessed | tf_op | source)
XLA Modules:
  0.0 47.0 jit_solution(6644964401421730777)
XLA Ops:
  0.0 45.7 %layer.1 = bf16[16,512]{1,0:T(8,128)(2,1)} custom-call(bf16[16,512]{1,0:T(8,128)(2,1)} %x_hbm.1, bf16[8192]{0:T(1024)(128)(2,1)} %gain_one_hbm.1, bf16[8192,512]{1,0:T(8,128)(2,1)} %q_hbm.1, bf16[512,8192]{1,0:T(8,128)(2,1)} %o_hbm.1, bf16[8192]{0:T(1024)(128)(2,1)} %gain_two_hbm.1, bf16[8192,896]{1,0:T(8,128)(2,1)} %gate_hbm.1, bf16[8192,896]{1,0:T(8,128)(2,1)} %up_hbm.1, ...), custom_call_target="tpu_custom_call" | custom-call | tf_op jit(solution)/shard_map/layer/pallas_call | solution.py:632
  45.7 1.3 %copy.12 = bf16[16,512]{1,0:T(8,128)(2,1)} copy(bf16[16,512]{1,0:T(8,128)(2,1)} %layer.1) | data formatting | bytes 32768

commit v3 on v2

--- a/solution.py
+++ b/solution.py
@@ -173,6 +173,7 @@
     part_two,
     got_two,
     own_ref,
+    raw,
     w_sem,
     in_sem,
     stage_sem,
@@ -336,7 +337,9 @@
         inverse = lax.rsqrt(mean + eps)
         for i in range(devices):
             part_gain = gain[i * cols : (i + 1) * cols].astype(jnp.float32).reshape(1, cols)
-            normed[i] = (values[i].astype(jnp.float32) * inverse * part_gain).astype(jnp.bfloat16)
+            normed[:, i * cols : (i + 1) * cols] = (
+                values[i].astype(jnp.float32) * inverse * part_gain
+            ).astype(jnp.bfloat16)
 
     with jax.named_scope("t_xgather"):
         gather_pass(*x_sems)
@@ -346,22 +349,11 @@
     norm(x_all, gain_one)
     with jax.named_scope("t_fetchq"):
         fetch_q.wait()
-    step = 4
-
-    def q_step(t, total):
-        for u in range(step):
-            i = t * step + u
-            total = total + jnp.dot(
-                normed[i],
-                q_w[pl.ds(pl.multiple_of(i * cols, cols), cols), :],
-                preferred_element_type=jnp.float32,
-            )
-        return total
 
     with jax.named_scope("t_qmm"):
-        queries = lax.fori_loop(
-            0, devices // step, q_step, jnp.zeros((rows, cols), jnp.float32)
-        ).astype(jnp.bfloat16)
+        queries = jnp.dot(normed[...], q_w[...], preferred_element_type=jnp.float32).astype(
+            jnp.bfloat16
+        )
         q_own[...] = jnp.concatenate(
             [queries[:, h * HEAD_DIM : (h + 1) * HEAD_DIM] for h in range(group)], axis=0
         )
@@ -483,7 +475,7 @@
             [ratio[h * rows : (h + 1) * rows] for h in range(group)], axis=1
         ).astype(jnp.bfloat16)
 
-    def scatter(values, weight, duo, duo_got, duo_send, duo_recv, part, got, send, recv):
+    def scatter(lag, values, weight, duo, duo_got, duo_send, duo_recv, part, got, send, recv):
         def product(to):
             return jnp.dot(
                 values,
@@ -503,42 +495,34 @@
                 chip_at(chips - 1 - s) * 2 + core,
             )
 
-        def turn_one(t, _):
-            @pl.when(t > 0)
-            def _():
-                give(2 * t - 2).start()
-                give(2 * t - 1).start()
-
-            first = product(chip_at(chips - 1 - 2 * t) * 2 + 1 - core)
-            second = product(chip_at(chips - 2 - 2 * t) * 2 + 1 - core)
-            duo[2 * t] = first
-            duo[2 * t + 1] = second
-            return 0
-
-        def turn_two(t, _):
-            @pl.when(t > 0)
-            def _():
-                post(2 * t - 2).start()
-                post(2 * t - 1).start()
-
-            first = product(chip_at(chips - 1 - 2 * t) * 2 + core)
-            second = product(chip_at(chips - 2 - 2 * t) * 2 + core)
-            give(2 * t).wait_recv()
-            give(2 * t + 1).wait_recv()
-            first = first + duo_got[2 * t]
-            second = second + duo_got[2 * t + 1]
-            part[2 * t] = first.astype(part.dtype)
-            part[2 * t + 1] = second.astype(part.dtype)
-            own_ref[...] = second
-            return 0
-
-        with jax.named_scope("t_prod1"):
-            lax.fori_loop(0, chips // 2, turn_one, 0)
-            give(chips - 2).start()
-            give(chips - 1).start()
-        with jax.named_scope("t_prod2"):
-            lax.fori_loop(0, chips // 2, turn_two, 0)
-            post(chips - 2).start()
+        def finish(s):
+            give(s).wait_recv()
+            both = raw[s] + duo_got[s]
+            if s == chips - 1:
+                own_ref[...] = both
+            else:
+                part[s] = both.astype(part.dtype)
+            if s > 0:
+                post(s - 1).start()
+
+        before = None
+        with jax.named_scope("t_prod"):
+            for turn in range(2 * chips):
+                s = turn % chips
+                to = chip_at(chips - 1 - s) * 2
+                now = product(to + 1 - core if turn < chips else to + core)
+                if turn > 0:
+                    store = duo if turn <= chips else raw
+                    store[(turn - 1) % chips] = before
+                if 2 <= turn < chips + 2:
+                    give(turn - 2).start()
+                if turn - chips >= lag:
+                    finish(turn - chips - lag)
+                before = now
+            raw[chips - 1] = before
+        with jax.named_scope("t_fin"):
+            for s in range(chips - lag, chips):
+                finish(s)
 
         whole(part.at[pl.ds(0, chips - 1)], recv).wait()
         total = own_ref[...]
@@ -555,7 +539,7 @@
     with jax.named_scope("t_fetcho"):
         fetch_o.wait()
     with jax.named_scope("t_scat1"):
-        attn_out = scatter(attended, o_w, *one)
+        attn_out = scatter(chips, attended, o_w, *one)
     stream = (x_all[me].astype(jnp.float32) + attn_out).astype(jnp.bfloat16)
     s_all[me] = stream
     gather_start(*s_sems)
@@ -566,25 +550,15 @@
     with jax.named_scope("t_fetchgu"):
         fetch_gate.wait()
         fetch_up.wait()
-    wide = gate_w.shape[1]
-
-    def ff_step(t, sums):
-        gate, upward = sums
-        for u in range(2):
-            i = t * 2 + u
-            at = pl.ds(pl.multiple_of(i * cols, cols), cols)
-            gate = gate + jnp.dot(normed[i], gate_w[at, :], preferred_element_type=jnp.float32)
-            upward = upward + jnp.dot(normed[i], up_w[at, :], preferred_element_type=jnp.float32)
-        return gate, upward
-
-    zeros = jnp.zeros((rows, wide), jnp.float32)
+
     with jax.named_scope("t_ffmm"):
-        gate, upward = lax.fori_loop(0, devices // 2, ff_step, (zeros, zeros))
+        gate = jnp.dot(normed[...], gate_w[...], preferred_element_type=jnp.float32)
+        upward = jnp.dot(normed[...], up_w[...], preferred_element_type=jnp.float32)
     hidden = (gate / (1.0 + jnp.exp(-gate)) * upward).astype(jnp.bfloat16)
     with jax.named_scope("t_fetchd"):
         fetch_down.wait()
     with jax.named_scope("t_scat2"):
-        down_out = scatter(hidden, down_w, *two)
+        down_out = scatter(chips // 2, hidden, down_w, *two)
     y_ref[...] = (s_all[me].astype(jnp.float32) + down_out).astype(jnp.bfloat16)
 
     with jax.named_scope("t_drain"):
@@ -646,7 +620,7 @@
             pltpu.VMEM((KV_HEADS, 1, rows), jnp.int32),
             exchange,
             exchange,
-            exchange,
+            pltpu.VMEM((rows, devices * cols), jnp.bfloat16),
             pltpu.VMEM((2, chips // 2, MASK_AT + rows, HEAD_DIM), jnp.bfloat16),
             pltpu.VMEM((chips, MASK_AT + rows, HEAD_DIM), jnp.bfloat16),
             pltpu.VMEM((chips, 2 * lines, BLOCK), jnp.float32),
@@ -656,6 +630,7 @@
             pieces,
             *([duo, duo, part, part] * 2),
             pltpu.VMEM((rows, cols), jnp.float32),
+            duo,
             dma((5,)),
             dma((4,)),
             dma(()),

time: 47.3 us -> 46.1 us (0.975)
  Pallas kernels: 45.7 us -> 44.6 us
    pallas_call x1, Pallas kernels: 45.7 us -> 44.6 us  [layer(): pl.pallas_call(layer_kernel, name='layer', out_shape=jax.ShapeDtypeStruct...]
where the time goes in v3:
time: 46.1 us; the launch traced here: 45.9 us
  Pallas kernels  44.6 us (97%)
  local copies, waits for them, and re-layouts  1.32 us (3%)
    pallas_call x1, Pallas kernels, layer(): pl.pallas_call(layer_kernel, name='layer', out_shape=jax.ShapeDtypeStruct...  44.6 us
    unnamed x1, local copies, waits for them, and re-layouts  1.32 us

profile of v3, /device:TPU:0, one launch (start us, length us, event | category | flops | bytes accessed | tf_op | source)
XLA Modules:
  0.0 45.9 jit_solution(3634700794661169931)
XLA Ops:
  0.0 44.6 %layer.1 = bf16[16,512]{1,0:T(8,128)(2,1)} custom-call(bf16[16,512]{1,0:T(8,128)(2,1)} %x_hbm.1, bf16[8192]{0:T(1024)(128)(2,1)} %gain_one_hbm.1, bf16[8192,512]{1,0:T(8,128)(2,1)} %q_hbm.1, bf16[512,8192]{1,0:T(8,128)(2,1)} %o_hbm.1, bf16[8192]{0:T(1024)(128)(2,1)} %gain_two_hbm.1, bf16[8192,896]{1,0:T(8,128)(2,1)} %gate_hbm.1, bf16[8192,896]{1,0:T(8,128)(2,1)} %up_hbm.1, ...), custom_call_target="tpu_custom_call" | custom-call | tf_op jit(solution)/shard_map/layer/pallas_call | solution.py:606
  44.6 1.3 %copy.12 = bf16[16,512]{1,0:T(8,128)(2,1)} copy(bf16[16,512]{1,0:T(8,128)(2,1)} %layer.1) | data formatting | bytes 32768
